TPU v7x, 128 devices: a whole 4x4x4 slice. The times are simulated.
128 devices in a mesh: dp: 8 (over x, core), fsdp: 16 (over z, y).
Axes of the slice: x: 4, y: 4, z: 4, core: 2. Of those that a mesh axis runs over, the one named last changes fastest.
Arguments:
- tokens: bfloat16 [65536, 1408], P(('dp', 'fsdp')), may hold values from -6 to 6
- image_of: int32 [65536], P(('dp', 'fsdp')), may hold values from 0 to 16383, as said below
- live: int32 [65536], P(('dp', 'fsdp')), may hold values from 0 to 1, as said below
- request_of: int32 [16384], P('dp'), may hold values from -1 to 63, as said below
- ln1_gain: float32 [1408], replicated, may hold values from 0.5 to 1.5
- ln1_shift: float32 [1408], replicated, may hold values from -3 to 3
- w_qkv: bfloat16 [1408, 4224], P('fsdp')
- b_qkv: float32 [4224], replicated, may hold values from -3 to 3
- w_out: bfloat16 [1408, 1408], P('fsdp'), may hold values from -0.15625 to 0.15625
- b_out: float32 [1408], replicated, may hold values from -3 to 3
- ln2_gain: float32 [1408], replicated, may hold values from 0.5 to 1.5
- ln2_shift: float32 [1408], replicated, may hold values from -3 to 3
- w_proj: bfloat16 [5632, 4096], P(None, 'fsdp'), may hold values from -0.078125 to 0.078125
- b_proj: float32 [4096], P('fsdp'), may hold values from -3 to 3
Outputs:
- features: bfloat16 [16384, 4096], P('dp', 'fsdp')
- peaks: float32 [64], replicated
Inputs may be any that keep to these rules, and one draw needn't show every extreme that they name: `image_of`: tokens come in aligned groups of 4 of one image; an image's tokens are consecutive and lie within one aligned block of 512 rows; numbers never fall along the rows; the last block's last group of 4 is an image of its own. Padding fills whole groups of 4 at the end of each aligned block of 512 rows, at most half of the block; the first group of every block is live and the last block has none; a padding token carries the image number of the token before it. `request_of`: -1 exactly on merged rows of padding; on the other rows request numbers never fall along the rows, and every request has some row.
All inputs are finite; a program needn't handle non-finite values.
Results may differ from a plain program's by a relative error of at most 0.012.
The roundings to bfloat16 on the way count: a program that leaves them out, or rounds other values in their place, can miss the bound.
Values may be sent and summed in bfloat16 or wider, within the bound.
A program may use at most 192 MiB of HBM per device.

v0:
```python
import jax
import jax.numpy as jnp
from jax import lax
from jax.sharding import PartitionSpec as P

HEADS = 16


def normalize(values, gain, shift):
    mean_value = jnp.mean(values, axis=-1, keepdims=True)
    centred = values - mean_value
    variance = jnp.mean(centred * centred, axis=-1, keepdims=True)
    return centred * lax.rsqrt(variance + 1e-06) * gain + shift


def attention(qkv, image_ids, live_flags, heads):
    count_rows = qkv.shape[0]
    width = qkv.shape[1] // 3
    head_size = width // heads
    scale = head_size ** (-0.5)
    queries = qkv[:, :width].reshape(count_rows, heads, head_size)
    keys_all = qkv[:, width : 2 * width].reshape(count_rows, heads, head_size)
    values_all = qkv[:, 2 * width :].reshape(count_rows, heads, head_size)
    block_rows = min(512, count_rows)
    blocks = count_rows // block_rows
    key_live = live_flags[None, :] == 1

    def one_block(items):
        block_queries, block_images = items
        scores = (
            jnp.einsum("qhe,khe->hqk", block_queries, keys_all, preferred_element_type=jnp.float32)
            * scale
        )
        allowed = (block_images[:, None] == image_ids[None, :]) & key_live
        scores = jnp.where(allowed[None], scores, jnp.float32(-1e30))
        top = jnp.max(scores, axis=-1, keepdims=True)
        expo = jnp.exp(scores - top)
        weights = (expo / jnp.sum(expo, axis=-1, keepdims=True)).astype(jnp.bfloat16)
        mixed = jnp.einsum("hqk,khe->qhe", weights, values_all, preferred_element_type=jnp.float32)
        return mixed.reshape(block_rows, width).astype(jnp.bfloat16)

    result = lax.map(
        one_block,
        (
            queries.reshape(blocks, block_rows, heads, head_size),
            image_ids.reshape(blocks, block_rows),
        ),
    )
    return result.reshape(count_rows, width)


def shards(
    tokens,
    image_of,
    live,
    request_of,
    ln1_gain,
    ln1_shift,
    w_qkv,
    b_qkv,
    w_out,
    b_out,
    ln2_gain,
    ln2_shift,
    w_proj,
    b_proj,
):
    count_rows = tokens.shape[0]
    width = tokens.shape[1]
    resid = tokens.astype(jnp.float32)
    normed = normalize(resid, ln1_gain, ln1_shift).astype(jnp.bfloat16)
    columns = normed
    mixed = jnp.dot(
        columns,
        lax.all_gather(w_qkv, "fsdp", axis=0, tiled=True),
        preferred_element_type=jnp.float32,
    )
    qkv = (mixed + b_qkv).astype(jnp.bfloat16)
    attended = attention(qkv, image_of, live, HEADS)
    columns = attended
    projected_out = jnp.dot(
        columns,
        lax.all_gather(w_out, "fsdp", axis=0, tiled=True),
        preferred_element_type=jnp.float32,
    )
    resid = resid + (projected_out + b_out)
    normed2 = normalize(resid, ln2_gain, ln2_shift).astype(jnp.bfloat16)
    merged = normed2.reshape(count_rows // 4, 4 * width)
    projected = (
        jnp.dot(
            lax.all_gather(merged, "fsdp", axis=0, tiled=True),
            w_proj,
            preferred_element_type=jnp.float32,
        )
        + b_proj
    )
    requests = lax.axis_size("dp") * lax.axis_size("fsdp") // 2
    columns_here = projected.shape[1]
    labels = jnp.arange(requests, dtype=jnp.int32)
    member = request_of[:, None] == labels[None, :]
    row_squares = jnp.sum(projected * projected, axis=1)
    row_top = jnp.max(projected, axis=1)
    sums_part = jnp.sum(jnp.where(member, row_squares[:, None], jnp.float32(0.0)), axis=0)
    entries_part = jnp.sum(member.astype(jnp.float32), axis=0) * jnp.float32(columns_here)
    top_part = jnp.max(jnp.where(member, row_top[:, None], jnp.float32(-jnp.inf)), axis=0)
    sumsq, entries = lax.psum((sums_part, entries_part), ("dp", "fsdp"))
    top = lax.pmax(top_part, ("dp", "fsdp"))
    rms = jnp.sqrt(sumsq / entries + 1e-06)
    valid = request_of >= 0
    row_rms = jnp.sum(jnp.where(member, rms[None, :], jnp.float32(0.0)), axis=1) + jnp.where(
        valid, 0.0, 1.0
    )
    features = jnp.where(valid[:, None], projected / row_rms[:, None], jnp.float32(0.0)).astype(
        jnp.bfloat16
    )
    peaks = top / rms
    return (features, peaks)


def solution(mesh):
    return jax.shard_map(
        shards,
        mesh=mesh,
        in_specs=(
            P(("dp", "fsdp"), None),
            P(("dp", "fsdp")),
            P(("dp", "fsdp")),
            P("dp"),
            P(),
            P(),
            P("fsdp", None),
            P(),
            P("fsdp", None),
            P(),
            P(),
            P(),
            P(None, "fsdp"),
            P("fsdp"),
        ),
        out_specs=(P("dp", "fsdp"), P()),
        check_vma=False,
    )
```

profile of v0, /device:TPU:1, one launch (start us, length us, event | category | flops | bytes accessed | tf_op | source)
XLA Modules:
  0.0 461.9 jit_solution(2938531197813447947)
XLA Ops:
  7.2 0.0 copy-start
  7.2 0.0 copy-start.6
  7.2 0.0 copy-start.5
  7.2 0.0 copy-start.9
  7.2 0.0 copy-start.8
  7.2 0.0 copy-start.7
  7.2 0.0 all-gather.4.cloned.1.call-start
  7.3 0.7 all-gather.4.cloned.1.call-update
  8.0 0.0 all-gather.6.cloned.1.call-start
  8.0 0.7 all-gather.6.cloned.1.call-update
  8.7 0.0 all-gather.8.cloned.1.call-start
  8.8 1.6 convert_reduce_fusion
  10.4 1.9 fusion.8
  12.3 0.0 copy-done.6
  12.3 0.0 copy-done.5
  12.3 0.2 compare_and_fusion
  12.6 87.9 %all-gather.4.cloned.1.call-done = bf16[1408,4224]{1,0:T(8,128)(2,1)} async-done(((bf16[88,4224]{1,0:T(8,128)(2,1)}), bf16[1408,4224]{1,0:T(8,128)(2,1)}) %all-gather.4.cloned.1.call-update) | async-done | bytes 11894800 | tf_op jit(solution)/shard_map/all_gather | solution.py:75
  100.5 0.0 copy-done.9
  100.5 0.0 copy-done.8
  100.5 0.0 copy-done.7
  100.5 12.4 %add_convert_fusion = bf16[512,4224]{1,0:T(8,128)(2,1)S(1)} fusion(bf16[1408,4224]{1,0:T(8,128)(2,1)} %all-gather.4.cloned.1.call-done, f32[4224]{0:T(1024)S(1)} %copy-done.7, bf16[512,1408]{1,0:T(8,128)(2,1)} %param.14, f32[1408]{0:T(1024)S(1)} %copy-done.8, f32[1408]{0:T(1024)S(1)} %copy-done.9, f32[512]{0:T(512)S(1)} %add_rsqrt_fusion.1, ...), kind=kOutput, calls=%fused_computation.5 | convolution fusion | flops 6098780160 | bytes 17694208 | tf_op jit(solution)/shard_map/dot_general | solution.py:73
  112.8 2.1 fusion.23
  115.0 2.6 copy.27
  117.6 2.5 copy.28
  120.1 2.6 copy.26
  122.7 11.0 %fusion.24 = (f32[16,512]{1,0:T(8,128)S(1)}, f32[16,512,512]{1,2,0:T(8,128)}) fusion(pred[512,512]{0,1:T(8,128)(4,1)S(1)} %compare_and_fusion, bf16[512,16,88]{0,2,1:T(8,128)(2,1)} %bitcast.17, bf16[512,16,88]{0,2,1:T(8,128)(2,1)} %bitcast.18), kind=kOutput, calls=%fused_computation.50 | convolution fusion | flops 754975232 | bytes 19955712 | tf_op jit(solution)/shard_map/while/body/eval_jaxpr/sub | solution.py:37
  133.7 0.0 copy-start.2
  133.7 8.9 %fusion.14 = bf16[16,88,512]{2,1,0:T(8,128)(2,1)} fusion(bf16[512,16,88]{0,2,1:T(8,128)(2,1)} %bitcast.19, f32[16,512,512]{1,2,0:T(8,128)} %get-tuple-element.46, f32[16,512]{1,0:T(8,128)S(1)} %get-tuple-element.45), kind=kOutput, calls=%fused_computation.26 | convolution fusion | flops 747307008 | bytes 19693568 | tf_op jit(solution)/shard_map/while/body/eval_jaxpr/hqk,khe->qhe/dot_general | solution.py:39
  142.5 10.3 %all-gather.6.cloned.1.call-done = bf16[1408,1408]{1,0:T(8,128)(2,1)} async-done(((bf16[88,1408]{1,0:T(8,128)(2,1)}), bf16[1408,1408]{1,0:T(8,128)(2,1)}) %all-gather.6.cloned.1.call-update) | async-done | bytes 3964944 | tf_op jit(solution)/shard_map/all_gather | solution.py:83
  152.9 0.0 copy-done.2
  152.9 5.9 %fusion.25 = (f32[512]{0:T(512)S(1)}, f32[512,1408]{1,0:T(8,128)S(1)}) fusion(f32[1408]{0:T(1024)S(1)} %copy-done.2, bf16[512,1408]{0,1:T(8,128)(2,1)} %bitcast.16, bf16[1408,1408]{1,0:T(8,128)(2,1)} %all-gather.6.cloned.1.call-done, bf16[512,1408]{1,0:T(8,128)(2,1)} %param.14), kind=kOutput, calls=%fused_computation.51 | convolution fusion | flops 2032926208 | bytes 9739776 | tf_op jit(solution)/shard_map/dot_general | solution.py:81
  158.8 0.0 copy-start.3
  158.8 0.0 copy-start.4
  158.8 0.4 multiply_reduce_fusion
  159.3 0.2 copy-done.3
  159.5 0.0 copy-done.4
  159.5 1.7 add_convert_fusion.1
  161.2 0.0 copy-start.10
  161.2 3.6 reshape.109
  164.8 0.0 all-gather.8.cloned.1.call-update
  164.8 0.0 copy-start.1
  164.8 143.3 %all-gather.8.cloned.1.call-done = bf16[2048,5632]{1,0:T(8,128)(2,1)} async-done(((bf16[128,5632]{1,0:T(8,128)(2,1)}), bf16[2048,5632]{1,0:T(8,128)(2,1)}) %all-gather.8.cloned.1.call-update) | async-done | bytes 23068688 | tf_op jit(solution)/shard_map/all_gather | solution.py:91
  308.2 0.0 copy-done
  308.2 0.0 copy-done.10
  308.2 12.5 %fusion.22 = (f32[2048]{0:T(1024)S(1)}, f32[2048]{0:T(1024)S(1)}, f32[2048,256]{0,1:T(8,128)}) fusion(f32[256]{0:T(256)S(1)} %copy-done.10, bf16[2048,5632]{1,0:T(8,128)(2,1)} %all-gather.8.cloned.1.call-done, bf16[5632,256]{1,0:T(8,128)(2,1)S(1)} %copy-done), kind=kOutput, calls=%fused_computation.48 | convolution fusion | flops 5907673088 | bytes 28066816 | tf_op jit(solution)/shard_map/dot_general | solution.py:90
  320.7 0.0 copy-done.1
  320.7 0.2 convert_reduce_fusion.1
  320.9 64.6 %all-reduce = (f32[64]{0:T(128)S(1)}, f32[64]{0:T(128)S(1)}) all-reduce(f32[64]{0:T(128)S(1)} %get-tuple-element.37, f32[64]{0:T(128)S(1)} %broadcast_multiply_fusion.2), channel_id=1, replica_groups=mesh['dp'=8,'fsdp'=16] {'dp','fsdp'}, use_global_device_ids=true, to_apply=%region_8.9 | all-reduce | flops 128 | bytes 1024 | tf_op jit(solution)/shard_map/psum | solution.py:106
  385.5 0.2 select_reduce_fusion
  385.7 64.1 %pmax.7 = f32[64]{0:T(128)S(1)} all-reduce(f32[64]{0:T(128)S(1)} %get-tuple-element.34), channel_id=1, replica_groups=mesh['dp'=8,'fsdp'=16] {'dp','fsdp'}, use_global_device_ids=true, to_apply=%region_14.15 | all-reduce | flops 64 | bytes 512 | tf_op jit(solution)/shard_map/pmax | solution.py:107
  449.8 0.5 div.47
  450.3 2.8 select_convert_fusion
  453.2 2.3 copy.30
  (8 shorter events, 0.0 us)
Async XLA Ops:
  7.2 301.0 %copy-start = (bf16[5632,256]{1,0:T(8,128)(2,1)S(1)}, bf16[5632,256]{1,0:T(8,128)(2,1)}, u32[]{:S(2)}) copy-start(bf16[5632,256]{1,0:T(8,128)(2,1)} %param.26) | copy-start | bytes 8650756
  7.2 5.1 %copy-start.6 = (s32[512]{0:T(512)S(1)}, s32[512]{0:T(512)}, u32[]{:S(2)}) copy-start(s32[512]{0:T(512)} %param.16) | copy-start | bytes 6148
  7.2 5.1 %copy-start.5 = (s32[512]{0:T(512)S(1)}, s32[512]{0:T(512)}, u32[]{:S(2)}) copy-start(s32[512]{0:T(512)} %param.15) | copy-start | bytes 6148
  7.2 93.3 %copy-start.9 = (f32[1408]{0:T(1024)S(1)}, f32[1408]{0:T(1024)}, u32[]{:S(2)}) copy-start(f32[1408]{0:T(1024)} %param.18) | copy-start | bytes 16900
  7.2 93.3 %copy-start.8 = (f32[1408]{0:T(1024)S(1)}, f32[1408]{0:T(1024)}, u32[]{:S(2)}) copy-start(f32[1408]{0:T(1024)} %param.19) | copy-start | bytes 16900
  7.2 93.3 %copy-start.7 = (f32[4224]{0:T(1024)S(1)}, f32[4224]{0:T(1024)}, u32[]{:S(2)}) copy-start(f32[4224]{0:T(1024)} %param.21) | copy-start | bytes 50692
  7.2 93.2 %all-gather.4.cloned.1.call-start = ((), (), s32[]{:S(2)}) async-start(), calls=%async_computation | async-start | bytes 12638208 | tf_op jit(solution)/shard_map/all_gather | solution.py:75
  8.0 144.9 %all-gather.6.cloned.1.call-start = ((), (), s32[]{:S(2)}) async-start(), calls=%async_computation.1 | async-start | bytes 4212736 | tf_op jit(solution)/shard_map/all_gather | solution.py:83
  8.7 299.4 %all-gather.8.cloned.1.call-start = ((), (), s32[]{:S(2)}) async-start(), calls=%async_computation.2 | async-start | bytes 24510464 | tf_op jit(solution)/shard_map/all_gather | solution.py:91
  133.7 19.2 %copy-start.2 = (f32[1408]{0:T(1024)S(1)}, f32[1408]{0:T(1024)}, u32[]{:S(2)}) copy-start(f32[1408]{0:T(1024)} %param.23) | copy-start | bytes 16900
  158.8 0.7 copy-start.3
  158.8 0.7 copy-start.4
  161.2 147.0 %copy-start.10 = (f32[256]{0:T(256)S(1)}, f32[256]{0:T(256)}, u32[]{:S(2)}) copy-start(f32[256]{0:T(256)} %param.27) | copy-start | bytes 3076
  164.8 155.8 %copy-start.1 = (s32[2048]{0:T(1024)S(1)}, s32[2048]{0:T(1024)}, u32[]{:S(2)}) copy-start(s32[2048]{0:T(1024)} %param.17) | copy-start | bytes 24580
Sparse Core Ops, SparseCore 0:
  10.2 90.2 all-gather.3
  102.6 50.2 all-gather.5
  164.9 143.1 all-gather.7
where the time goes:
time: 462 us
  waiting for transfers between devices  243 us (53%)
  blocking collectives  129 us (28%)
  matrix products  50.6 us (11%)
  local copies, waits for them, and re-layouts  16 us (3%)
  between operations  13.9 us (3%)
  other arithmetic  9.62 us (2%)
    all_gather x1, waiting for transfers between devices, shards(): lax.all_gather(merged, 'fsdp', axis=0, tiled=True)  143 us
    all_gather x1, waiting for transfers between devices, shards(): lax.all_gather(w_qkv, 'fsdp', axis=0, tiled=True)  87.9 us
    psum x1, blocking collectives, shards(): sumsq, entries = lax.psum((sums_part, entries_part), ('dp', 'fsdp'))  64.6 us
    pmax x1, blocking collectives, shards(): top = lax.pmax(top_part, ('dp', 'fsdp'))  64.1 us
    dot_general x1, matrix products, shards(): jnp.dot(lax.all_gather(merged, 'fsdp', axis=0, tiled=True), w_proj, prefe...  12.5 us
    dot_general x1, matrix products, shards(): jnp.dot(columns, lax.all_gather(w_qkv, 'fsdp', axis=0, tiled=True), prefe...  12.4 us
    sub x1, matrix products, one_block(): expo = jnp.exp(scores - top)  11 us
    all_gather x1, waiting for transfers between devices, shards(): lax.all_gather(w_out, 'fsdp', axis=0, tiled=True)  10.3 us
  transfers between devices with their start and end apart: 3, of which 3 were waited for; matrix products, arithmetic and copies ran while one was open for 10% of the time, Pallas kernels for 0%

commit v1 on v0

--- a/solution.py
+++ b/solution.py
@@ -88,7 +88,9 @@
     merged = normed2.reshape(count_rows // 4, 4 * width)
     projected = (
         jnp.dot(
-            lax.all_gather(merged, "fsdp", axis=0, tiled=True),
+            jnp.concatenate(
+                lax.all_to_all(jnp.stack([merged] * lax.axis_size("fsdp")), "fsdp", 0, 0), axis=0
+            ),
             w_proj,
             preferred_element_type=jnp.float32,
         )

time: 462 us -> 581 us (1.26)
  blocking collectives: 129 us -> 385 us
  waiting for transfers between devices: 243 us -> 99.7 us
    all_to_all x0 -> x1, blocking collectives: none -> 257 us  [shards(): lax.all_to_all(jnp.stack([merged] * lax.axis_size('fsdp')), 'fsdp', 0, 0)]
    all_gather x1 -> x0, waiting for transfers between devices: 143 us -> none  [shards(): lax.all_gather(merged, 'fsdp', axis=0, tiled=True)]
    another operation x0 -> x2, local copies, waits for them, and re-layouts: none -> 8.36 us  [shards(): jnp.stack([merged] * lax.axis_size('fsdp'))]
  transfers between devices with their start and end apart: 3 -> 2, of which waited for: 3 -> 2; matrix products, arithmetic and copies ran while one was open for 10% -> 8% of each run, Pallas kernels for 0% -> 0%
where the time goes in v1:
time: 581 us; the launch traced here: 580 us
  blocking collectives  385 us (66%)
  waiting for transfers between devices  99.7 us (17%)
  matrix products  50.7 us (9%)
  local copies, waits for them, and re-layouts  20.8 us (4%)
  between operations  14.2 us (2%)
  other arithmetic  9.62 us (2%)
    all_to_all x1, blocking collectives, shards(): lax.all_to_all(jnp.stack([merged] * lax.axis_size('fsdp')), 'fsdp', 0, 0)  257 us
    all_gather x1, waiting for transfers between devices, shards(): lax.all_gather(w_qkv, 'fsdp', axis=0, tiled=True)  88 us
    psum x1, blocking collectives, shards(): sumsq, entries = lax.psum((sums_part, entries_part), ('dp', 'fsdp'))  64.2 us
    pmax x1, blocking collectives, shards(): top = lax.pmax(top_part, ('dp', 'fsdp'))  63.8 us
    dot_general x1, matrix products, shards(): jnp.dot(jnp.concatenate(lax.all_to_all(jnp.stack([merged] * lax.axis_size...  12.5 us
    dot_general x1, matrix products, shards(): jnp.dot(columns, lax.all_gather(w_qkv, 'fsdp', axis=0, tiled=True), prefe...  12.4 us
  transfers between devices with their start and end apart: 2, of which 2 were waited for; matrix products, arithmetic and copies ran while one was open for 8% of the time, Pallas kernels for 0%

profile of v1, /device:TPU:1, one launch (start us, length us, event | category | flops | bytes accessed | tf_op | source)
XLA Modules:
  0.0 579.9 jit_solution(2521560944470038648)
XLA Ops:
  7.2 0.0 copy-start
  7.2 0.0 copy-start.6
  7.2 0.0 copy-start.5
  7.2 0.0 copy-start.7
  7.2 0.0 copy-start.8
  7.2 0.0 copy-start.9
  7.2 0.0 all-gather.3.cloned.1.call-start
  7.3 0.7 all-gather.3.cloned.1.call-update
  8.0 0.0 all-gather.5.cloned.1.call-start
  8.0 0.7 all-gather.5.cloned.1.call-update
  8.7 1.6 convert_reduce_fusion
  10.3 1.9 fusion.8
  12.2 0.0 copy-done.6
  12.3 0.0 copy-done.5
  12.3 0.2 compare_and_fusion
  12.5 88.0 %all-gather.3.cloned.1.call-done = bf16[1408,4224]{1,0:T(8,128)(2,1)} async-done(((bf16[88,4224]{1,0:T(8,128)(2,1)}), bf16[1408,4224]{1,0:T(8,128)(2,1)}) %all-gather.3.cloned.1.call-update) | async-done | bytes 11894800 | tf_op jit(solution)/shard_map/all_gather | solution.py:75
  100.5 0.0 copy-done.7
  100.5 0.0 copy-done.8
  100.5 0.0 copy-done.9
  100.5 12.4 %add_convert_fusion = bf16[512,4224]{1,0:T(8,128)(2,1)S(1)} fusion(bf16[1408,4224]{1,0:T(8,128)(2,1)} %all-gather.3.cloned.1.call-done, f32[4224]{0:T(1024)S(1)} %copy-done.7, bf16[512,1408]{1,0:T(8,128)(2,1)} %param.14, f32[1408]{0:T(1024)S(1)} %copy-done.8, f32[1408]{0:T(1024)S(1)} %copy-done.9, f32[512]{0:T(512)S(1)} %add_rsqrt_fusion.1, ...), kind=kOutput, calls=%fused_computation.5 | convolution fusion | flops 6098780160 | bytes 17694208 | tf_op jit(solution)/shard_map/dot_general | solution.py:73
  112.8 2.2 fusion.23
  115.0 2.6 copy.28
  117.6 2.5 copy.27
  120.1 2.6 copy.26
  122.7 11.0 %fusion.24 = (f32[16,512]{1,0:T(8,128)S(1)}, f32[16,512,512]{1,2,0:T(8,128)}) fusion(pred[512,512]{0,1:T(8,128)(4,1)S(1)} %compare_and_fusion, bf16[512,16,88]{0,2,1:T(8,128)(2,1)} %bitcast.20, bf16[512,16,88]{0,2,1:T(8,128)(2,1)} %bitcast.19), kind=kOutput, calls=%fused_computation.50 | convolution fusion | flops 754975232 | bytes 19955712 | tf_op jit(solution)/shard_map/while/body/eval_jaxpr/sub | solution.py:37
  133.7 0.0 copy-start.2
  133.7 8.9 %fusion.14 = bf16[16,88,512]{2,1,0:T(8,128)(2,1)} fusion(bf16[512,16,88]{0,2,1:T(8,128)(2,1)} %bitcast.21, f32[16,512,512]{1,2,0:T(8,128)} %get-tuple-element.46, f32[16,512]{1,0:T(8,128)S(1)} %get-tuple-element.45), kind=kOutput, calls=%fused_computation.26 | convolution fusion | flops 747307008 | bytes 19693568 | tf_op jit(solution)/shard_map/while/body/eval_jaxpr/hqk,khe->qhe/dot_general | solution.py:39
  142.6 10.3 %all-gather.5.cloned.1.call-done = bf16[1408,1408]{1,0:T(8,128)(2,1)} async-done(((bf16[88,1408]{1,0:T(8,128)(2,1)}), bf16[1408,1408]{1,0:T(8,128)(2,1)}) %all-gather.5.cloned.1.call-update) | async-done | bytes 3964944 | tf_op jit(solution)/shard_map/all_gather | solution.py:83
  152.9 0.0 copy-done.2
  152.9 5.9 %fusion.25 = (f32[512]{0:T(512)S(1)}, f32[512,1408]{1,0:T(8,128)S(1)}) fusion(f32[1408]{0:T(1024)S(1)} %copy-done.2, bf16[512,1408]{0,1:T(8,128)(2,1)} %bitcast.18, bf16[1408,1408]{1,0:T(8,128)(2,1)} %all-gather.5.cloned.1.call-done, bf16[512,1408]{1,0:T(8,128)(2,1)} %param.14), kind=kOutput, calls=%fused_computation.51 | convolution fusion | flops 2032926208 | bytes 9739776 | tf_op jit(solution)/shard_map/dot_general | solution.py:81
  158.8 0.0 copy-start.3
  158.8 0.0 copy-start.4
  158.8 0.4 multiply_reduce_fusion
  159.3 0.2 copy-done.3
  159.5 0.0 copy-done.4
  159.5 1.7 add_convert_fusion.1
  161.2 3.6 stack_reshape.2
  164.8 4.8 stack.3
  169.6 0.0 copy-start.10
  169.6 257.0 %all_to_all.5 = bf16[16,128,5632]{2,1,0:T(8,128)(2,1)} all-to-all(bf16[16,128,5632]{2,1,0:T(8,128)(2,1)S(1)} %stack.3), channel_id=1, replica_groups=mesh['dp'=8,'fsdp'=16] {'fsdp'}, dimensions={0} | all-to-all | bytes 46137344 | tf_op jit(solution)/shard_map/all_to_all | solution.py:92
  426.6 0.0 copy-done
  426.6 0.0 copy-done.10
  426.6 0.0 copy-start.1
  426.6 12.5 %fusion.22 = (f32[2048]{0:T(1024)S(1)}, f32[2048]{0:T(1024)S(1)}, f32[2048,256]{0,1:T(8,128)}) fusion(f32[256]{0:T(256)S(1)} %copy-done.10, bf16[2048,5632]{1,0:T(8,128)(2,1)} %bitcast.17, bf16[5632,256]{1,0:T(8,128)(2,1)S(1)} %copy-done), kind=kOutput, calls=%fused_computation.48 | convolution fusion | flops 5907673088 | bytes 28066816 | tf_op jit(solution)/shard_map/dot_general | solution.py:90
  439.1 0.0 copy-done.1
  439.1 0.2 convert_reduce_fusion.1
  439.3 64.2 %all-reduce = (f32[64]{0:T(128)S(1)}, f32[64]{0:T(128)S(1)}) all-reduce(f32[64]{0:T(128)S(1)} %get-tuple-element.37, f32[64]{0:T(128)S(1)} %broadcast_multiply_fusion.2), channel_id=1, replica_groups=mesh['dp'=8,'fsdp'=16] {'dp','fsdp'}, use_global_device_ids=true, to_apply=%region_8.9 | all-reduce | flops 128 | bytes 1024 | tf_op jit(solution)/shard_map/psum | solution.py:108
  503.5 0.2 select_reduce_fusion
  503.7 63.8 %pmax.7 = f32[64]{0:T(128)S(1)} all-reduce(f32[64]{0:T(128)S(1)} %get-tuple-element.34), channel_id=1, replica_groups=mesh['dp'=8,'fsdp'=16] {'dp','fsdp'}, use_global_device_ids=true, to_apply=%region_14.15 | all-reduce | flops 64 | bytes 512 | tf_op jit(solution)/shard_map/pmax | solution.py:109
  567.5 0.5 div.47
  568.0 2.8 select_convert_fusion
  570.8 2.3 copy.30
  (8 shorter events, 0.0 us)
Async XLA Ops:
  7.2 419.4 %copy-start = (bf16[5632,256]{1,0:T(8,128)(2,1)S(1)}, bf16[5632,256]{1,0:T(8,128)(2,1)}, u32[]{:S(2)}) copy-start(bf16[5632,256]{1,0:T(8,128)(2,1)} %param.26) | copy-start | bytes 8650756
  7.2 5.0 copy-start.6
  7.2 5.1 copy-start.5
  7.2 93.3 %copy-start.7 = (f32[4224]{0:T(1024)S(1)}, f32[4224]{0:T(1024)}, u32[]{:S(2)}) copy-start(f32[4224]{0:T(1024)} %param.21) | copy-start | bytes 50692
  7.2 93.3 %copy-start.8 = (f32[1408]{0:T(1024)S(1)}, f32[1408]{0:T(1024)}, u32[]{:S(2)}) copy-start(f32[1408]{0:T(1024)} %param.19) | copy-start | bytes 16900
  7.2 93.3 %copy-start.9 = (f32[1408]{0:T(1024)S(1)}, f32[1408]{0:T(1024)}, u32[]{:S(2)}) copy-start(f32[1408]{0:T(1024)} %param.18) | copy-start | bytes 16900
  7.2 93.2 %all-gather.3.cloned.1.call-start = ((), (), s32[]{:S(2)}) async-start(), calls=%async_computation.1 | async-start | bytes 12638208 | tf_op jit(solution)/shard_map/all_gather | solution.py:75
  8.0 144.9 %all-gather.5.cloned.1.call-start = ((), (), s32[]{:S(2)}) async-start(), calls=%async_computation.2 | async-start | bytes 4212736 | tf_op jit(solution)/shard_map/all_gather | solution.py:83
  133.7 19.2 %copy-start.2 = (f32[1408]{0:T(1024)S(1)}, f32[1408]{0:T(1024)}, u32[]{:S(2)}) copy-start(f32[1408]{0:T(1024)} %param.23) | copy-start | bytes 16900
  158.8 0.7 copy-start.3
  158.8 0.7 copy-start.4
  169.6 257.0 %copy-start.10 = (f32[256]{0:T(256)S(1)}, f32[256]{0:T(256)}, u32[]{:S(2)}) copy-start(f32[256]{0:T(256)} %param.27) | copy-start | bytes 3076
  426.6 12.5 %copy-start.1 = (s32[2048]{0:T(1024)S(1)}, s32[2048]{0:T(1024)}, u32[]{:S(2)}) copy-start(s32[2048]{0:T(1024)} %param.17) | copy-start | bytes 24580
Sparse Core Ops, SparseCore 0:
  10.2 90.2 all-gather.2
  102.6 50.2 all-gather.4
